TPU v7x, 256 devices: a whole 4x4x8 slice. The times are simulated.
256 devices in a mesh: occ: 8 (over y_lo, x), vir: 32 (over y_hi, z, core).
Axes of the slice: x: 4, y: 4 (y_hi: 2, y_lo: 2; y = y_hi * 2 + y_lo), z: 8, core: 2. Of those that a mesh axis runs over, the one named last changes fastest.
Arguments:
- factors: bfloat16 [256, 1024, 2048], P(None, 'vir', 'occ'), may hold values from -0.125 to 0.125
- e_occ: float32 [256], replicated, may hold values from -2 to -0.3
- e_vir: float32 [1024], replicated, may hold values from 0.1 to 3
- i_sub: int32 [3], replicated, may hold values from 0 to 1
- j_row: int32 [3], replicated, may hold values from 0 to 255
Outputs:
- density: float32 [256, 1024, 2048], P(None, 'vir', 'occ')
All inputs are finite; a program needn't handle non-finite values.
Results may differ from a plain program's by a relative error of at most 0.0022.
Values may be sent and summed in bfloat16 or wider, within the bound.
A program may use at most 128 MiB of HBM per device.

v0:
```python
import jax
import jax.numpy as jnp
from jax import lax
from jax.sharding import PartitionSpec as P

IBK = 16
STEPS = 3


def from_root(shard, axis, root):
    mine = lax.axis_index(axis) == root
    return lax.psum(jnp.where(mine, shard, jnp.zeros_like(shard)), axis)


def pair_terms(accumulator, row_block, energy_rows, energy_own, energy_pair, column_piece, e_vir):
    integrals = jnp.einsum(
        "iap,bp->iab", row_block, column_piece, preferred_element_type=jnp.float32
    )
    denominator = (
        energy_own[None, :, None] + e_vir[None, None, :] - energy_rows[:, None, None] - energy_pair
    )
    amplitude = (-integrals / denominator).astype(jnp.bfloat16)
    return accumulator + jnp.einsum(
        "iab,bp->iap", amplitude, column_piece, preferred_element_type=jnp.float32
    )


def shards(factors, e_occ, e_vir, i_sub, j_row):
    regrouped = lax.all_to_all(factors, "occ", split_axis=0, concat_axis=2, tiled=True)
    owned, vir_own, aux_total = regrouped.shape
    occ_rank = lax.axis_index("occ")
    vir_rank = lax.axis_index("vir")
    energy_own = lax.dynamic_slice_in_dim(e_vir, vir_rank * vir_own, vir_own, 0)
    density = jnp.zeros((owned, vir_own, aux_total), jnp.float32)
    offsets = []
    row_blocks = []
    energy_list = []
    pair_slabs = []
    pair_energies = []
    for step_index in range(STEPS):
        offset = i_sub[step_index] * IBK
        j_index = j_row[step_index]
        owner = j_index // owned
        own_slab = lax.dynamic_index_in_dim(regrouped, j_index % owned, 0, keepdims=False)
        pair_slab = from_root(own_slab, "occ", owner)
        offsets.append(offset)
        row_blocks.append(lax.dynamic_slice_in_dim(regrouped, offset, IBK, 0))
        energy_list.append(lax.dynamic_slice_in_dim(e_occ, occ_rank * owned + offset, IBK, 0))
        pair_slabs.append(pair_slab)
        pair_energies.append(e_occ[j_index])
    for step_index in range(STEPS):
        previous = lax.dynamic_slice_in_dim(density, offsets[step_index], IBK, 0)
        updated = pair_terms(
            previous,
            row_blocks[step_index],
            energy_list[step_index],
            energy_own,
            pair_energies[step_index],
            lax.all_gather(pair_slabs[step_index], "vir", axis=0, tiled=True),
            e_vir,
        )
        density = lax.dynamic_update_slice_in_dim(density, updated, offsets[step_index], 0)
    return lax.all_to_all(density, "occ", split_axis=2, concat_axis=0, tiled=True)


def solution(mesh):
    placed = (P(None, "vir", "occ"), P(), P(), P(), P())
    return jax.shard_map(
        shards, mesh=mesh, in_specs=placed, out_specs=P(None, "vir", "occ"), check_vma=False
    )
```

profile of v0, /device:TPU:1, one launch (start us, length us, event | category | flops | bytes accessed | tf_op | source)
XLA Modules:
  0.0 679.4 jit_solution(2114121080004834413)
XLA Ops:
  6.5 6.0 all-to-all-start
  12.5 0.0 all-reduce.3.cloned.1.call-start
  12.6 0.6 fusion.64
  20.4 41.8 %all-to-all-done = bf16[256,32,256]{2,1,0:T(8,128)(2,1)} async-done(((bf16[256,32,256]{2,1,0:T(8,128)(2,1)}), bf16[256,32,256]{2,1,0:T(8,128)(2,1)}, u32[]{:S(2)}, u32[]{:S(2)}) %all-to-all-start) | async-done | bytes 4194336 | tf_op jit(solution)/shard_map/all_to_all | solution.py:29
  62.2 8.5 %copy.12 = bf16[8,32,32,256]{3,0,2,1:T(8,128)(2,1)} copy(bf16[8,32,32,256]{3,2,1,0:T(8,128)(2,1)} %bitcast) | data formatting | bytes 8388608 | tf_op jit(solution)/shard_map/all_to_all | solution.py:29
  70.7 7.4 %all_to_all.29 = bf16[32,32,2048]{2,1,0:T(8,128)(2,1)} reshape(bf16[32,32,8,256]{3,2,1,0:T(8,128)(2,1)} %bitcast.62) | data formatting | bytes 8388608 | tf_op jit(solution)/shard_map/all_to_all | solution.py:29
  78.1 1.8 select_bitcast_fusion
  79.9 0.0 all-gather.4.cloned.1.call-start
  80.0 89.0 %all-reduce.3.cloned.1.call-done = (bf16[32,2048]{1,0:T(8,128)(2,1)}, bf16[32,2048]{1,0:T(8,128)(2,1)}, bf16[32,2048]{1,0:T(8,128)(2,1)}) async-done(((bf16[32,2048]{1,0:T(8,128)(2,1)}, bf16[32,2048]{1,0:T(8,128)(2,1)}, bf16[32,2048]{1,0:T(8,128)(2,1)}), (bf16[32,2048]{1,0:T(8,128)(2,1)}, bf16[32,2048]{1,0:T(8,128)(2,1)}, bf16[32,2048]{1,0:T(8,128)(2,1)})) %all-reduce.3.cloned.1.call-update) | async-done | bytes 393232 | tf_op jit(solution)/shard_map/psum | solution.py:12
  169.0 0.0 all-gather.6.cloned.1.call-start
  169.1 0.7 all-gather.6.cloned.1.call-update
  169.8 0.2 all-gather.8.cloned.1.call-start
  170.0 0.3 all-gather.8.cloned.1.call-update
  170.3 0.7 fusion.63
  176.4 0.1 dynamic_slice.48
  176.5 0.6 fusion.62
  177.1 0.1 fusion.61
  177.2 0.1 broadcast_add_fusion
  177.3 86.9 %all-gather.4.cloned.1.call-done = bf16[1024,2048]{1,0:T(8,128)(2,1)} async-done(((bf16[32,2048]{1,0:T(8,128)(2,1)}), bf16[1024,2048]{1,0:T(8,128)(2,1)}) %all-gather.4.cloned.1.call-update) | async-done | bytes 4194320 | tf_op jit(solution)/shard_map/all_gather | solution.py:59
  264.1 4.5 broadcast_in_dim.2
  268.6 11.2 %fusion.12 = f32[32,32,2048]{2,1,0:T(8,128)} fusion(f32[32,32,2048]{2,1,0:T(8,128)} %broadcast_in_dim.2, s32[]{:T(128)S(6)} %select_n.99, bf16[1024,2048]{1,0:T(8,128)(2,1)} %all-gather.4.cloned.1.call-done, bf16[32,32,2048]{2,1,0:T(8,128)(2,1)} %all_to_all.29, f32[]{:T(128)} %bitcast.6, f32[16]{0:T(128)S(1)} %get-tuple-element.13, ...), kind=kOutput, calls=%fused_computation.15 | convolution fusion | flops 4297588736 | bytes 14812736 | tf_op jit(solution)/shard_map/iab,bp->iap/dot_general | solution.py:23
  279.8 70.5 %all-gather.6.cloned.1.call-done = bf16[1024,2048]{1,0:T(8,128)(2,1)} async-done(((bf16[32,2048]{1,0:T(8,128)(2,1)}), bf16[1024,2048]{1,0:T(8,128)(2,1)}) %all-gather.6.cloned.1.call-update) | async-done | bytes 4194320 | tf_op jit(solution)/shard_map/all_gather | solution.py:59
  350.2 12.4 %add_dynamic-update-slice_fusion.1 = f32[32,32,2048]{2,1,0:T(8,128)} fusion(f32[32,32,2048]{2,1,0:T(8,128)} %fusion.12, s32[]{:T(128)S(6)} %select_n.109, bf16[1024,2048]{1,0:T(8,128)(2,1)} %all-gather.6.cloned.1.call-done, bf16[32,32,2048]{2,1,0:T(8,128)(2,1)} %all_to_all.29, f32[]{:T(128)} %bitcast.11, f32[16]{0:T(128)S(1)} %get-tuple-element.12, ...), kind=kOutput, calls=%fused_computation.14 | convolution fusion | flops 4298637312 | bytes 19007040 | tf_op jit(solution)/shard_map/iab,bp->iap/dot_general | solution.py:23
  362.7 73.5 %all-gather.8.cloned.1.call-done = bf16[1024,2048]{1,0:T(8,128)(2,1)} async-done(((bf16[32,2048]{1,0:T(8,128)(2,1)}), bf16[1024,2048]{1,0:T(8,128)(2,1)}) %all-gather.8.cloned.1.call-update) | async-done | bytes 4194320 | tf_op jit(solution)/shard_map/all_gather | solution.py:59
  436.2 12.5 %add_dynamic-update-slice_fusion = f32[32,32,2048]{2,1,0:T(8,128)} fusion(f32[32,32,2048]{2,1,0:T(8,128)} %add_dynamic-update-slice_fusion.1, s32[]{:T(128)S(6)} %select_n.118, bf16[1024,2048]{1,0:T(8,128)(2,1)} %all-gather.8.cloned.1.call-done, bf16[32,32,2048]{2,1,0:T(8,128)(2,1)} %all_to_all.29, f32[]{:T(128)} %bitcast.16, f32[16]{0:T(128)S(1)} %get-tuple-element.11, ...), kind=kOutput, calls=%fused_computation.13 | convolution fusion | flops 4298637312 | bytes 19007040 | tf_op jit(solution)/shard_map/iab,bp->iap/dot_general | solution.py:23
  448.6 26.3 %copy.9 = f32[32,32,2048]{1,0,2:T(8,128)} copy(f32[32,32,2048]{2,1,0:T(8,128)} %add_dynamic-update-slice_fusion) | data formatting | bytes 16777216 | tf_op jit(solution)/shard_map/dynamic_update_slice | solution.py:62
  474.9 20.5 %reshape.53 = f32[8,1,262144]{2,1,0:T(1,128)} reshape(f32[2048,32,32]{2,1,0:T(8,128)} %bitcast.60) | data formatting | bytes 16777216
  495.4 100.2 %all_to_all.36 = f32[8,1,262144]{2,1,0:T(1,128)} all-to-all(f32[8,1,262144]{2,1,0:T(1,128)} %reshape.53), channel_id=1, replica_groups=mesh['occ'=8,'vir'=32] {'occ'}, dimensions={0} | all-to-all | bytes 16777216 | tf_op jit(solution)/shard_map/all_to_all | solution.py:63
  595.7 0.5 broadcast.49
  596.2 26.4 %reduce = f32[8,262144]{1,0:T(8,128)} reduce(f32[8,1,262144]{2,1,0:T(1,128)} %all_to_all.36, f32[]{:T(128)} %broadcast.49), dimensions={1}, to_apply=%all_to_all.30.reduce_sub_computation | reduce | bytes 16777220 | tf_op jit(solution)/shard_map/all_to_all | solution.py:63
  622.6 25.3 %reshape.54 = f32[2048,32,32]{2,1,0:T(8,128)} reshape(f32[8,262144]{1,0:T(8,128)} %reduce) | data formatting | bytes 16777216
  647.9 25.1 %copy.10 = f32[8,32,32,256]{3,2,1,0:T(8,128)} copy(f32[8,32,32,256]{2,1,3,0:T(8,128)} %bitcast.61) | data formatting | bytes 16777216 | tf_op jit(solution)/shard_map/all_to_all | solution.py:63
  (10 shorter events, 0.0 us)
Async XLA Ops:
  6.5 6.0 copy-start.1
  6.5 55.7 %all-to-all-start = ((bf16[256,32,256]{2,1,0:T(8,128)(2,1)}), bf16[256,32,256]{2,1,0:T(8,128)(2,1)}, u32[]{:S(2)}, u32[]{:S(2)}) async-start(bf16[256,32,256]{2,1,0:T(8,128)(2,1)} %param.5), calls=%async_computation | async-start | bytes 8388608 | tf_op jit(solution)/shard_map/all_to_all | solution.py:29
  12.5 156.5 %all-reduce.3.cloned.1.call-start = ((), (), s32[]{:S(2)}) async-start(), calls=%async_computation.5 | async-start | bytes 786432 | tf_op jit(solution)/shard_map/psum | solution.py:12
  70.7 99.7 %copy-start.2 = (s32[3]{0:T(128)S(1)}, s32[3]{0:T(128)}, u32[]{:S(2)}) copy-start(s32[3]{0:T(128)} %param.8) | copy-start | bytes 40
  70.7 105.7 %copy-start.3 = (f32[1024]{0:T(1024)S(1)}, f32[1024]{0:T(1024)}, u32[]{:S(2)}) copy-start(f32[1024]{0:T(1024)} %param.7) | copy-start | bytes 12292
  70.7 105.8 %copy-start = (f32[256]{0:T(256)S(1)}, f32[256]{0:T(256)}, u32[]{:S(2)}) copy-start(f32[256]{0:T(256)} %param.6) | copy-start | bytes 3076
  79.9 184.2 %all-gather.4.cloned.1.call-start = ((), (), s32[]{:S(2)}) async-start(), calls=%async_computation.2 | async-start | bytes 4325376 | tf_op jit(solution)/shard_map/all_gather | solution.py:59
  169.0 181.2 %all-gather.6.cloned.1.call-start = ((), (), s32[]{:S(2)}) async-start(), calls=%async_computation.3 | async-start | bytes 4325376 | tf_op jit(solution)/shard_map/all_gather | solution.py:59
  169.8 266.4 %all-gather.8.cloned.1.call-start = ((), (), s32[]{:S(2)}) async-start(), calls=%async_computation.4 | async-start | bytes 4325376 | tf_op jit(solution)/shard_map/all_gather | solution.py:59
Sparse Core Ops, SparseCore 0:
  80.0 88.8 all-reduce.2
  171.8 92.3 all-gather.3
  266.9 83.2 all-gather.5
  352.9 83.2 all-gather.7
where the time goes:
time: 681 us; the launch traced here: 679 us
  waiting for transfers between devices  363 us (53%)
  local copies, waits for them, and re-layouts  120 us (18%)
  blocking collectives  100 us (15%)
  matrix products  36.1 us (5%)
  other arithmetic  28.3 us (4%)
  between operations  25.8 us (4%)
    all_gather x3, waiting for transfers between devices, shards(): lax.all_gather(pair_slabs[step_index], 'vir', axis=0, tiled=True)  231 us
    all_to_all x1, blocking collectives, shards(): lax.all_to_all(density, 'occ', split_axis=2, concat_axis=0, tiled=True)  100 us
    psum x1, waiting for transfers between devices, from_root(): return lax.psum(jnp.where(mine, shard, jnp.zeros_like(shard)), axis)  89 us
    unnamed x10, local copies, waits for them, and re-layouts  45.8 us
    all_to_all x1, waiting for transfers between devices, shards(): lax.all_to_all(factors, 'occ', split_axis=0, concat_axis=2, tiled=True)  41.8 us
    dot_general x3, matrix products, pair_terms(): jnp.einsum('iab,bp->iap', amplitude, column_piece, preferred_element_type...  36.1 us
    all_to_all x1, other arithmetic, shards(): lax.all_to_all(density, 'occ', split_axis=2, concat_axis=0, tiled=True)  26.4 us
    dynamic_update_slice x1, local copies, waits for them, and re-layouts, shards(): lax.dynamic_update_slice_in_dim(density, updated, offsets[step_index], 0)  26.3 us
  transfers between devices with their start and end apart: 5, of which 5 were waited for; matrix products, arithmetic and copies ran while one was open for 4% of the time, Pallas kernels for 0%

commit v1 on v0

v1 whole, which is shorter than its diff:
```python
import jax
import jax.numpy as jnp
from jax import lax
from jax.experimental import pallas as pl
from jax.experimental.pallas import tpu as pltpu
from jax.sharding import PartitionSpec as P

MESH = pl.DeviceIdType.MESH
F32 = jnp.float32
BF16 = jnp.bfloat16

STEPS = 3
IBK = 16
OCC = 8
VIR = 32
AB = 32
PB = 256
CHUNKS = 2
KB = IBK // CHUNKS
M = KB * AB
NB = 256
JB = VIR * AB // NB
VB = NB // AB


def rotate(index, shift, size):
    return lax.rem(index + (shift + size), size)


def kernel(
    i_sub, j_row, e_occ, e_vir, factors, own_pair, out,
    pair, rows0, rows1, er, amp, acc, snd0, snd1,
    in_s, in_r, gat_s, gat_r, z_s, z_r, f_s, f_r, p_s, p_r, o_s, o_r, loc,
):
    o, v = lax.axis_index("occ"), lax.axis_index("vir")
    yl, x = o // 4, lax.rem(o, 4)
    yh, z, core = v // 16, lax.rem(v // 2, 8), lax.rem(v, 2)
    rows, snd = (rows0, rows1), (snd0, snd1)

    def occ_at(d):
        return lax.rem(yl + d // 4, 2) * 4 + lax.rem(x + lax.rem(d, 4), 4)

    def occ_from(d):
        return lax.rem(yl + d // 4, 2) * 4 + lax.rem(x + 4 - lax.rem(d, 4), 4)

    def block_at(side, dz):
        high = 1 - yh if side else yh
        return high * 16 + rotate(z, dz, 8) * 2 + core

    far = ((1 - yl) * 4 + x, (1 - yh) * 16 + z * 2 + core)
    mate = (o, v + 1 - 2 * core)
    up = (o, block_at(0, 1))
    down = (o, block_at(0, -1))

    barrier = pltpu.get_barrier_semaphore()
    for d in range(1, OCC):
        pl.semaphore_signal(barrier, inc=1, device_id=(occ_at(d), v), device_id_type=MESH)
    for device in (far, mate, up, down):
        pl.semaphore_signal(barrier, inc=1, device_id=device, device_id_type=MESH)
    pl.semaphore_wait(barrier, OCC + 3)

    sends = []

    def send(src, dst, ssem, rsem, device):
        copy = pltpu.make_async_remote_copy(
            src_ref=src, dst_ref=dst, send_sem=ssem, recv_sem=rsem, device_id=device, device_id_type=MESH
        )
        copy.start()
        sends.append(copy)

    def arrived(ref, rsem):
        pltpu.make_async_copy(ref, ref, rsem).wait()

    own_copies = [pltpu.make_async_copy(own_pair, pair.at[:, v, o], loc.at[0])]
    own_copies += [pltpu.make_async_copy(factors.at[o, :, pl.ds(c * KB, KB)], rows[c].at[o], loc.at[1 + c]) for c in range(CHUNKS)]
    for copy in own_copies:
        copy.start()

    order = (1, 3, 4, 5, 7, 2, 6)
    for d in order:
        send(own_pair, pair.at[:, v, o], gat_s.at[d], gat_r.at[d], (occ_at(d), v))
    for c in range(CHUNKS):
        for u in range(2):
            for d in order:
                r = occ_at(d)
                send(factors.at[r, u, pl.ds(c * KB, KB)], rows[c].at[o, u], in_s.at[c, u, d], in_r.at[c, u, d], (r, v))

    lanes = lax.broadcasted_iota(jnp.int32, (AB, 128), 1)
    subl = lax.broadcasted_iota(jnp.int32, (AB, 128), 0)
    mine = e_vir[pl.ds(v // 4, 1), :]
    own_e = jnp.sum(jnp.where(lanes == subl + lax.rem(v, 4) * AB, mine, 0.0), axis=1, keepdims=True)
    for s in range(STEPS):
        e_pair = e_occ[j_row[s]]
        first = o * 32 + i_sub[s] * IBK
        for k in range(IBK):
            er[s, k * AB : (k + 1) * AB, :] = jnp.broadcast_to(own_e - e_occ[first + k] - e_pair, (AB, 128))

    streams = ((0, 0), (0, 1), (1, 0), (2, 0))
    half = {1: pl.ds(0, 4), -1: pl.ds(4, 4)}

    def view(s, b, part):
        return pair.at[s, b] if part is None else pair.at[s, b, part]

    def to_ring(n, direction, hop, b, part):
        s = streams[n][0]
        side = 0 if direction == 1 else 1
        ref = view(s, b, part)
        send(ref, ref, z_s.at[n, side, hop], z_r.at[n, side, hop], up if direction == 1 else down)

    def to_mate(s, side, slot, b, part):
        ref = view(s, b, part)
        send(ref, ref, p_s.at[s, side, slot], p_r.at[s, side, slot], mate)

    def to_far(s, slot, b, part):
        ref = view(s, b, part)
        send(ref, ref, f_s.at[s, slot], f_r.at[s, slot], far)

    def slot_of(direction, hop):
        return hop if direction == 1 else 4 + hop

    own_copies[0].wait()
    for d in range(1, OCC):
        arrived(pair.at[:, v, occ_from(d)], gat_r.at[d])
    for s in range(STEPS):
        to_far(s, 0, v, None)
    for n in (0, 2, 3):
        for direction in (1, -1):
            to_ring(n, direction, 1, v, None)
    for s in range(STEPS):
        to_mate(s, 0, 0, v, None)
    other = block_at(1, 0)
    for s in range(STEPS):
        arrived(view(s, other, None), f_r.at[s, 0])
        if s == 0:
            for direction in (1, -1):
                to_ring(1, direction, 1, other, None)
        to_mate(s, 1, 0, other, None)

    def ring_step(n, hop):
        s, side = streams[n]
        for direction in (1, -1):
            b = block_at(side, -direction * hop)
            part = half[direction] if hop == 4 else None
            arrived(view(s, b, part), z_r.at[n, 0 if direction == 1 else 1, hop])
            if hop < 4:
                to_ring(n, direction, hop + 1, b, half[direction] if hop == 3 else None)
            if s > 0:
                to_far(s, slot_of(direction, hop), b, part)
            to_mate(s, side, slot_of(direction, hop), b, part)

    def far_step(s, hop):
        for direction in (1, -1):
            b = block_at(1, -direction * hop)
            part = half[direction] if hop == 4 else None
            arrived(view(s, b, part), f_r.at[s, slot_of(direction, hop)])
            to_mate(s, 1, slot_of(direction, hop), b, part)

    def mate_done(s):
        for side in range(2):
            for slot in range(9):
                direction, hop = (1, slot) if slot <= 4 else (-1, slot - 4)
                b = block_at(side, -direction * hop) + 1 - 2 * core
                part = half[direction] if hop == 4 else None
                arrived(view(s, b, part), p_r.at[s, side, slot])

    def rows_done(c):
        own_copies[1 + c].wait()
        for u in range(2):
            for d in range(1, OCC):
                arrived(rows[c].at[occ_from(d), u], in_r.at[c, u, d])

    def integrals(c, s):
        sub = i_sub[s]
        column = er[s, pl.ds(c * M, M), :]
        column = jnp.concatenate([column] * (NB // 128), axis=1)

        def body(j, carry):
            left = jnp.concatenate([rows[c][r, sub].reshape(M, PB) for r in range(OCC)], axis=1)
            right = jnp.concatenate([pair[s, pl.ds(j * VB, VB), r].reshape(NB, PB) for r in range(OCC)], axis=1)
            value = lax.dot_general(left, right, (((1,), (1,)), ((), ())), preferred_element_type=F32)
            row = jnp.concatenate([e_vir[pl.ds(j * 2 + h, 1), :] for h in range(2)], axis=1)
            amp[j] = (-value / (column + row)).astype(BF16)
            return carry

        lax.fori_loop(0, JB, body, 0, unroll=2)

    def density(c, s):
        sub = i_sub[s]

        def body(d, carry):
            r = occ_at(d)
            left = jnp.concatenate([amp[j] for j in range(JB)], axis=1)
            value = jnp.dot(left, pair[s, :, r].reshape(VIR * AB, PB), preferred_element_type=F32)
            for u in range(2):
                term = jnp.where(sub == u, value, 0.0)
                if s == 0:
                    acc[u, d] = term
                elif s < STEPS - 1:
                    acc[u, d] = acc[u, d] + term
                else:
                    snd[c][d, u] = (acc[u, d] + term).astype(BF16).reshape(KB, AB, PB)
            return carry

        lax.fori_loop(0, OCC, body, 0, unroll=2)

    def send_out(c):
        for d in order:
            for u in range(2):
                send(snd[c].at[d, u], out.at[o, u, pl.ds(c * KB, KB)], o_s.at[c, u, d], o_r.at[c, u, d], (occ_at(d), v))
        copy = pltpu.make_async_copy(snd[c].at[0], out.at[o, :, pl.ds(c * KB, KB)], loc.at[3 + c])
        copy.start()
        return copy

    for hop in range(1, 5):
        ring_step(0, hop)
        ring_step(1, hop)
        if hop > 1:
            far_step(1, hop - 1)
        ring_step(2, hop)
        if hop > 1:
            far_step(2, hop - 1)
        ring_step(3, hop)
        if hop == 4:
            mate_done(0)
            rows_done(0)
            integrals(0, 0)
            density(0, 0)
    far_step(1, 4)
    far_step(2, 4)
    mate_done(1)
    integrals(0, 1)
    density(0, 1)
    mate_done(2)
    integrals(0, 2)
    density(0, 2)
    last = [send_out(0)]
    rows_done(1)
    for s in range(STEPS):
        integrals(1, s)
        density(1, s)
    last.append(send_out(1))
    for copy in last:
        copy.wait()
    for c in range(CHUNKS):
        for u in range(2):
            for d in range(1, OCC):
                arrived(out.at[occ_from(d), u, pl.ds(c * KB, KB)], o_r.at[c, u, d])
    for copy in sends:
        copy.wait_send()


def shards(factors, e_occ, e_vir, i_sub, j_row):
    own_pair = jnp.stack(
        [lax.dynamic_index_in_dim(factors, j_row[s], 0, keepdims=False) for s in range(STEPS)]
    )
    dma = pltpu.SemaphoreType.DMA
    smem, vmem, hbm = (pl.BlockSpec(memory_space=m) for m in (pltpu.SMEM, pltpu.VMEM, pl.ANY))
    result = pl.pallas_call(
        kernel,
        out_shape=jax.ShapeDtypeStruct((OCC, 2, IBK, AB, PB), BF16),
        in_specs=[smem, smem, smem, vmem, hbm, hbm],
        out_specs=hbm,
        scratch_shapes=[
            pltpu.VMEM((STEPS, VIR, OCC, AB, PB), BF16),
            pltpu.VMEM((OCC, 2, KB, AB, PB), BF16),
            pltpu.VMEM((OCC, 2, KB, AB, PB), BF16),
            pltpu.VMEM((STEPS, IBK * AB, 128), F32),
            pltpu.VMEM((JB, M, NB), BF16),
            pltpu.VMEM((2, OCC, M, PB), F32),
            pltpu.VMEM((OCC, 2, KB, AB, PB), BF16),
            pltpu.VMEM((OCC, 2, KB, AB, PB), BF16),
            dma((CHUNKS, 2, OCC)), dma((CHUNKS, 2, OCC)),
            dma((OCC,)), dma((OCC,)),
            dma((4, 2, 5)), dma((4, 2, 5)),
            dma((STEPS, 9)), dma((STEPS, 9)),
            dma((STEPS, 2, 9)), dma((STEPS, 2, 9)),
            dma((CHUNKS, 2, OCC)), dma((CHUNKS, 2, OCC)),
            dma((5,)),
        ],
        compiler_params=pltpu.CompilerParams(
            collective_id=0, has_side_effects=True, vmem_limit_bytes=48 * 2**20
        ),
        name="pair_densities",
    )(
        i_sub, j_row, e_occ, e_vir.reshape(8, 128),
        factors.reshape(OCC, 2, IBK, AB, PB), own_pair,
    )
    return result.reshape(factors.shape).astype(F32)


def solution(mesh):
    placed = (P(None, "vir", "occ"), P(), P(), P(), P())
    return jax.shard_map(
        shards, mesh=mesh, in_specs=placed, out_specs=P(None, "vir", "occ"), check_vma=False
    )
```

time: 681 us -> 153 us (0.22)
  waiting for transfers between devices: 363 us -> 0 us
  Pallas kernels: 0 us -> 138 us
  local copies, waits for them, and re-layouts: 120 us -> 4.86 us
  blocking collectives: 100 us -> 0 us
  matrix products: 36.1 us -> 0 us
  other arithmetic: 28.3 us -> 4.75 us
  between operations: 25.8 us -> 5.71 us
    all_gather x3 -> x0, waiting for transfers between devices: 231 us -> none  [shards(): lax.all_gather(pair_slabs[step_index], 'vir', axis=0, tiled=True)]
    pallas_call x0 -> x1, Pallas kernels: none -> 138 us  [shards(): pl.pallas_call(kernel, out_shape=jax.ShapeDtypeStruct((OCC, 2, IBK, AB, P...]
    all_to_all x1 -> x0, blocking collectives: 100 us -> none  [shards(): lax.all_to_all(density, 'occ', split_axis=2, concat_axis=0, tiled=True)]
    psum x1 -> x0, waiting for transfers between devices: 89 us -> none  [from_root(): return lax.psum(jnp.where(mine, shard, jnp.zeros_like(shard)), axis)]
    unnamed x10 -> x8, local copies, waits for them, and re-layouts: 45.8 us -> 2.67 us
    all_to_all x1 -> x0, waiting for transfers between devices: 41.8 us -> none  [shards(): lax.all_to_all(factors, 'occ', split_axis=0, concat_axis=2, tiled=True)]
    all_to_all x4 -> x0, local copies, waits for them, and re-layouts: 41.5 us -> none  [the longest x2 25.6 us: shards(): lax.all_to_all(density, 'occ', split_axis=2, concat_axis=0, tiled=True)]
    dot_general x3 -> x0, matrix products: 36.1 us -> none  [pair_terms(): jnp.einsum('iab,bp->iap', amplitude, column_piece, preferred_element_type...]
  transfers between devices with their start and end apart: 5 -> 0, of which waited for: 5 -> 0; matrix products, arithmetic and copies ran while one was open for 4% -> 0% of each run, Pallas kernels for 0% -> 0%
where the time goes in v1:
time: 153 us
  Pallas kernels  138 us (90%)
  between operations  5.71 us (4%)
  local copies, waits for them, and re-layouts  4.86 us (3%)
  other arithmetic  4.75 us (3%)
    pallas_call x1, Pallas kernels, shards(): pl.pallas_call(kernel, out_shape=jax.ShapeDtypeStruct((OCC, 2, IBK, AB, P...  138 us
    convert_element_type x1, other arithmetic, shards(): return result.reshape(factors.shape).astype(F32)  4.74 us

profile of v1, /device:TPU:1, one launch (start us, length us, event | category | flops | bytes accessed | tf_op | source)
XLA Modules:
  0.0 152.9 jit_solution(15457615514616675973)
XLA Ops:
  0.0 1.4 fusion
  7.1 0.8 constant_dynamic-slice_fusion.2
  7.9 0.0 copy-start
  7.9 0.6 copy-done
  8.6 0.0 copy-start.1
  8.6 0.7 copy-done.1
  9.2 0.0 copy-start.2
  9.2 0.7 copy-done.2
  9.9 0.0 copy-start.3
  9.9 0.7 copy-done.3
  10.6 137.6 %pair_densities.1 = bf16[8,2,16,32,256]{4,3,2,1,0:T(8,128)(2,1)S(1)} custom-call(s32[3]{0:T(128)S(1)} %copy-done.3, s32[3]{0:T(128)S(1)} %copy-done, f32[256]{0:T(256)S(1)} %copy-done.2, f32[8,128]{1,0:T(8,128)S(1)} %bitcast.8, bf16[8,2,16,32,256]{4,3,2,1,0:T(8,128)(2,1)} %bitcast.9, bf16[3,32,256]{2,1,0:T(8,128)(2,1)S(1)} %pad_maximum_fusion.own_pair), custom_call_target="tpu_custom_call" | custom-call | tf_op jit(solution)/shard_map/pair_densities/pallas_call | solution.py:258
  148.2 4.7 %bitcast_convert_fusion = f32[256,32,256]{2,1,0:T(8,128)} fusion(bf16[8,2,16,32,256]{4,3,2,1,0:T(8,128)(2,1)S(1)} %pair_densities.1), kind=kLoop, calls=%fused_computation | loop fusion | flops 2097152 | bytes 12582912 | tf_op jit(solution)/shard_map/convert_element_type | solution.py:288
  (1 shorter events, 0.0 us)
Async XLA Ops:
  7.9 0.7 copy-start
  8.6 0.7 copy-start.1
  9.2 0.7 copy-start.2
  9.9 0.7 copy-start.3

commit v2 on v1

v2 whole, which is shorter than its diff:
```python
import jax
import jax.numpy as jnp
from jax import lax
from jax.experimental import pallas as pl
from jax.experimental.pallas import tpu as pltpu
from jax.sharding import PartitionSpec as P

MESH = pl.DeviceIdType.MESH
F32 = jnp.float32
BF16 = jnp.bfloat16

STEPS = 3
IBK = 16
OCC = 8
VIR = 32
AB = 32
PB = 256
CHUNKS = 2
KB = IBK // CHUNKS
M = KB * AB
NB = 256
JB = VIR * AB // NB
FARTOP = 6


def rotate(index, shift, size):
    return lax.rem(index + (shift + size), size)


def kernel(
    i_sub_hbm, j_row_hbm, e_occ_hbm, e_vir_hbm, factors, out,
    i_sub, j_row, e_occ, e_vir, e_turned, e_group, er,
    held, own_pair, pair, rows0, rows1, amp, acc, snd0, snd1,
    in_s, in_r, gat_s, gat_r, z_s, z_r, f_s, f_r, p_s, p_r, o_s, o_r, loc,
):
    o, v = lax.axis_index("occ"), lax.axis_index("vir")
    yl, x = o // 4, lax.rem(o, 4)
    yh, z, core = v // 16, lax.rem(v // 2, 8), lax.rem(v, 2)
    rows, snd = (rows0, rows1), (snd0, snd1)

    def occ_at(d):
        return lax.rem(yl + d // 4, 2) * 4 + lax.rem(x + lax.rem(d, 4), 4)

    def occ_from(d):
        return lax.rem(yl + d // 4, 2) * 4 + lax.rem(x + 4 - lax.rem(d, 4), 4)

    def block_at(side, dz):
        high = 1 - yh if side else yh
        return high * 16 + rotate(z, dz, 8) * 2 + core

    far = ((1 - yl) * 4 + x, (1 - yh) * 16 + z * 2 + core)
    mate = (o, v + 1 - 2 * core)
    up = (o, block_at(0, 1))
    down = (o, block_at(0, -1))

    small = [
        pltpu.make_async_copy(a, b, loc.at[n])
        for n, (a, b) in enumerate(((j_row_hbm, j_row), (i_sub_hbm, i_sub), (e_occ_hbm, e_occ), (e_vir_hbm, e_vir)))
    ]
    small[0].start()
    whole = pltpu.make_async_copy(factors, held, loc.at[4])
    whole.start()
    for copy in small[1:]:
        copy.start()

    barrier = pltpu.get_barrier_semaphore()
    for d in range(1, OCC):
        pl.semaphore_signal(barrier, inc=1, device_id=(occ_at(d), v), device_id_type=MESH)
    for device in (far, mate, up, down):
        pl.semaphore_signal(barrier, inc=1, device_id=device, device_id_type=MESH)

    for copy in small:
        copy.wait()
    whole.wait()
    for s in range(STEPS):
        j = j_row[s]
        own_pair[s] = held[j // 32, lax.rem(j // 16, 2), lax.rem(j, 16)]
    pl.semaphore_wait(barrier, OCC + 3)

    sends = []

    def send(src, dst, ssem, rsem, device):
        copy = pltpu.make_async_remote_copy(
            src_ref=src, dst_ref=dst, send_sem=ssem, recv_sem=rsem, device_id=device, device_id_type=MESH
        )
        copy.start()
        sends.append(copy)

    def arrived(ref, rsem):
        pltpu.make_async_copy(ref, ref, rsem).wait()

    order = (1, 3, 4, 5, 7, 2, 6)
    for d in order:
        send(own_pair, pair.at[:, v, o], gat_s.at[d], gat_r.at[d], (occ_at(d), v))
    own_copies = [pltpu.make_async_copy(own_pair, pair.at[:, v, o], loc.at[5])]
    own_copies += [pltpu.make_async_copy(held.at[o, :, pl.ds(c * KB, KB)], rows[c].at[o], loc.at[6 + c]) for c in range(CHUNKS)]
    for copy in own_copies:
        copy.start()
    for c in range(CHUNKS):
        for u in range(2):
            for d in order:
                r = occ_at(d)
                send(factors.at[r, u, pl.ds(c * KB, KB)], rows[c].at[o, u], in_s.at[c, u, d], in_r.at[c, u, d], (r, v))

    e_turned[...] = pltpu.roll(e_vir[...], 64, 1)
    lanes = lax.broadcasted_iota(jnp.int32, (AB, 128), 1)
    subl = lax.broadcasted_iota(jnp.int32, (AB, 128), 0)
    mine = e_vir[pl.ds(v // 4, 1), :]
    own_e = jnp.sum(jnp.where(lanes == subl + lax.rem(v, 4) * AB, mine, 0.0), axis=1, keepdims=True)
    for s in range(STEPS):
        e_pair = e_occ[j_row[s]]
        first = o * 32 + i_sub[s] * IBK
        for k in range(IBK):
            er[s, k * AB : (k + 1) * AB, :] = jnp.broadcast_to(own_e - e_occ[first + k] - e_pair, (AB, 128))

    def places(g):
        return (z, rotate(z, 4, 8)) if g == 0 else (rotate(z, -g, 8), rotate(z, g, 8))

    lane = lax.broadcasted_iota(jnp.int32, (1, 128), 1)
    for g in range(JB):
        za, zb = places(g)
        for high in range(2):
            ra, rb = pl.ds(high * 4 + za // 2, 1), pl.ds(high * 4 + zb // 2, 1)
            ea = jnp.where(lax.rem(za, 2) == 0, e_vir[ra, :], e_turned[ra, :])
            eb = jnp.where(lax.rem(zb, 2) == 1, e_vir[rb, :], e_turned[rb, :])
            e_group[g, :, high * 128 : (high + 1) * 128] = jnp.where(lane < 64, ea, eb)

    streams = ((1, 0, 0, 8), (2, 0, 0, 8), (0, 0, 0, 8), (0, 1, 0, 8), (2, 1, FARTOP, 8))
    far_top = {0: 8, 1: 8, 2: FARTOP}

    def view(s, b, lo, hi):
        return pair.at[s, b] if (lo, hi) == (0, OCC) else pair.at[s, b, pl.ds(lo, hi - lo)]

    def part(direction, hop, lo, hi):
        if hop < 4:
            return lo, hi
        mid = (lo + hi) // 2
        return (lo, mid) if direction == 1 else (mid, hi)

    def to_ring(n, direction, hop, b):
        s, _, lo, hi = streams[n]
        side = 0 if direction == 1 else 1
        ref = view(s, b, *part(direction, hop, lo, hi))
        send(ref, ref, z_s.at[n, side, hop], z_r.at[n, side, hop], up if direction == 1 else down)

    def to_mate(kind, slot, s, b, lo, hi):
        ref = view(s, b, lo, hi)
        send(ref, ref, p_s.at[kind, slot], p_r.at[kind, slot], mate)

    def to_far(s, slot, b, lo, hi):
        hi = hi if slot == 0 else min(hi, far_top[s])
        if hi <= lo:
            return
        ref = view(s, b, lo, hi)
        send(ref, ref, f_s.at[s, slot], f_r.at[s, slot], far)

    def slot_of(direction, hop):
        return hop if direction == 1 else 4 + hop

    own_copies[0].wait()
    for d in range(1, OCC):
        arrived(pair.at[:, v, occ_from(d)], gat_r.at[d])
    for s in (0, 2, 1):
        to_far(s, 0, v, 0, 8)
    for n in range(3):
        for direction in (1, -1):
            to_ring(n, direction, 1, v)
    for n in range(3):
        to_mate(n, 0, streams[n][0], v, 0, 8)
    other = block_at(1, 0)
    for s, n in ((0, 3), (2, 4), (1, None)):
        arrived(view(s, other, 0, 8), f_r.at[s, 0])
        if n is not None:
            for direction in (1, -1):
                to_ring(n, direction, 1, other)
        to_mate(4 + s, 0, s, other, 0, 8)

    def ring_step(n, hop):
        s, side, lo, hi = streams[n]
        for direction in (1, -1):
            b = block_at(side, -direction * hop)
            slot = slot_of(direction, hop)
            p = part(direction, hop, lo, hi)
            arrived(view(s, b, *p), z_r.at[n, 0 if direction == 1 else 1, hop])
            if hop < 4:
                to_ring(n, direction, hop + 1, b)
            if s > 0 and side == 0:
                to_far(s, slot, b, *p)
            to_mate(7 if n == 4 else n, slot, s, b, *p)

    def far_step(s, hop):
        for direction in (1, -1):
            b = block_at(1, -direction * hop)
            slot = slot_of(direction, hop)
            lo, hi = part(direction, hop, 0, 8)
            hi = min(hi, far_top[s])
            if hi <= lo:
                continue
            arrived(view(s, b, lo, hi), f_r.at[s, slot])
            to_mate(4 + s, slot, s, b, lo, hi)

    def mate_done(kind, hops):
        s, side, lo, hi = streams[kind] if kind < 4 else (streams[4] if kind == 7 else (kind - 4, 1, 0, far_top[kind - 4]))
        for hop in hops:
            for direction in (1, -1) if hop else (1,):
                b = block_at(side, -direction * hop) + 1 - 2 * core
                p = part(direction, hop, lo, hi)
                if 4 <= kind < 7:
                    p = part(direction, hop, 0, 8)
                    p = (p[0], min(p[1], hi) if hop else 8)
                slot = slot_of(direction, hop)
                if p[0] < p[1]:
                    arrived(view(s, b, *p), p_r.at[kind, slot])

    def mate_all(s, hops):
        if s == 0:
            mate_done(2, hops)
            mate_done(3, [h for h in hops if h])
            mate_done(4, [h for h in hops if not h])
        else:
            mate_done(s - 1, hops)
            mate_done(4 + s, hops)
            if s == 2 and FARTOP < 8:
                mate_done(7, [h for h in hops if h])

    def rows_done(c):
        own_copies[1 + c].wait()
        for u in range(2):
            for d in range(1, OCC):
                arrived(rows[c].at[occ_from(d), u], in_r.at[c, u, d])

    def pieces(s, g, r):
        za, zb = places(g)
        return jnp.concatenate(
            [pair[s, pl.ds(high * 16 + zz * 2, 2), r].reshape(2 * AB, PB) for high in range(2) for zz in (za, zb)], axis=0
        )

    def integrals(c, s, g):
        column = er[s, pl.ds(c * M, M), :]
        column = jnp.concatenate([column] * (NB // 128), axis=1)
        sub = i_sub[s]
        left = jnp.concatenate([rows[c][r, sub].reshape(M, PB) for r in range(OCC)], axis=1)
        right = jnp.concatenate([pieces(s, g, r) for r in range(OCC)], axis=1)
        value = lax.dot_general(left, right, (((1,), (1,)), ((), ())), preferred_element_type=F32)
        amp[s, g] = (-value / (column + e_group[g])).astype(BF16)

    def density(c, s):
        sub = i_sub[s]

        def part_of(d):
            r = occ_at(d)
            left = jnp.concatenate([amp[s, g] for g in range(JB)], axis=1)
            right = jnp.concatenate([pieces(s, g, r) for g in range(JB)], axis=0)
            value = jnp.dot(left, right, preferred_element_type=F32)
            return [jnp.where(sub == u, value, 0.0) for u in range(2)]

        if s < STEPS - 1:
            def body(d, carry):
                for u, term in enumerate(part_of(d)):
                    acc[u, d] = term if s == 0 else acc[u, d] + term
                return carry

            lax.fori_loop(0, OCC, body, 0, unroll=4)
            return
        for d in order + (0,):
            for u, term in enumerate(part_of(d)):
                snd[c][d, u] = (acc[u, d] + term).astype(BF16).reshape(KB, AB, PB)
                if d:
                    send(snd[c].at[d, u], out.at[o, u, pl.ds(c * KB, KB)], o_s.at[c, u, d], o_r.at[c, u, d], (occ_at(d), v))
        last.append(pltpu.make_async_copy(snd[c].at[0], out.at[o, :, pl.ds(c * KB, KB)], loc.at[8 + c]))
        last[-1].start()

    last = []
    for hop in range(1, 5):
        for n in range(5 if FARTOP < 8 else 4):
            if n == 4 and hop > 1:
                far_step(1, hop - 1)
            ring_step(n, hop)
        if FARTOP == 8 and hop > 1:
            far_step(1, hop - 1)
        if hop > 1:
            far_step(2, hop - 1)
        if hop == 3:
            rows_done(0)
            mate_all(0, [1, 2])
            for s in (1, 2):
                mate_all(s, [1])
            for s, g in ((0, 1), (0, 2), (1, 1), (2, 1)):
                integrals(0, s, g)
    mate_all(0, [3])
    integrals(0, 0, 3)
    for s in (1, 2):
        mate_all(s, [2])
        integrals(0, s, 2)
    mate_all(0, [0, 4])
    integrals(0, 0, 0)
    far_step(1, 4)
    far_step(2, 4)
    density(0, 0)
    for s in (1, 2):
        mate_all(s, [3])
        integrals(0, s, 3)
        mate_all(s, [0, 4])
        integrals(0, s, 0)
        density(0, s)
    rows_done(1)
    for s in range(STEPS):
        for g in range(JB):
            integrals(1, s, g)
        density(1, s)
    for copy in last:
        copy.wait()
    for c in range(CHUNKS):
        for u in range(2):
            for d in range(1, OCC):
                arrived(out.at[occ_from(d), u, pl.ds(c * KB, KB)], o_r.at[c, u, d])
    for copy in sends:
        copy.wait_send()


def shards(factors, e_occ, e_vir, i_sub, j_row):
    dma = pltpu.SemaphoreType.DMA
    hbm = pl.BlockSpec(memory_space=pltpu.HBM)
    result = pl.pallas_call(
        kernel,
        out_shape=jax.ShapeDtypeStruct((OCC, 2, IBK, AB, PB), BF16),
        in_specs=[hbm] * 5,
        out_specs=pl.BlockSpec(memory_space=pl.ANY),
        scratch_shapes=[
            pltpu.SMEM((STEPS,), jnp.int32),
            pltpu.SMEM((STEPS,), jnp.int32),
            pltpu.SMEM((256,), F32),
            pltpu.VMEM((8, 128), F32),
            pltpu.VMEM((8, 128), F32),
            pltpu.VMEM((JB, 1, NB), F32),
            pltpu.VMEM((STEPS, IBK * AB, 128), F32),
            pltpu.VMEM((OCC, 2, IBK, AB, PB), BF16),
            pltpu.VMEM((STEPS, AB, PB), BF16),
            pltpu.VMEM((STEPS, VIR, OCC, AB, PB), BF16),
            pltpu.VMEM((OCC, 2, KB, AB, PB), BF16),
            pltpu.VMEM((OCC, 2, KB, AB, PB), BF16),
            pltpu.VMEM((STEPS, JB, M, NB), BF16),
            pltpu.VMEM((2, OCC, M, PB), F32),
            pltpu.VMEM((OCC, 2, KB, AB, PB), BF16),
            pltpu.VMEM((OCC, 2, KB, AB, PB), BF16),
            dma((CHUNKS, 2, OCC)), dma((CHUNKS, 2, OCC)),
            dma((OCC,)), dma((OCC,)),
            dma((5, 2, 5)), dma((5, 2, 5)),
            dma((STEPS, 9)), dma((STEPS, 9)),
            dma((8, 9)), dma((8, 9)),
            dma((CHUNKS, 2, OCC)), dma((CHUNKS, 2, OCC)),
            dma((10,)),
        ],
        compiler_params=pltpu.CompilerParams(
            collective_id=0, has_side_effects=True, vmem_limit_bytes=67_043_328
        ),
        name="pair_densities",
    )(i_sub, j_row, e_occ, e_vir.reshape(8, 128), factors.reshape(OCC, 2, IBK, AB, PB))
    return result.reshape(factors.shape).astype(F32)


def solution(mesh):
    placed = (P(None, "vir", "occ"), P(), P(), P(), P())
    return jax.shard_map(
        shards, mesh=mesh, in_specs=placed, out_specs=P(None, "vir", "occ"), check_vma=False
    )
```

time: 153 us -> 130 us (0.85)
  the two profiles are of different devices: /device:TPU:1 before, /device:TPU:30 now
where the time goes in v2:
time: 130 us
  Pallas kernels  124 us (95%)
  other arithmetic  6.66 us (5%)
    pallas_call x1, Pallas kernels, shards(): pl.pallas_call(kernel, out_shape=jax.ShapeDtypeStruct((OCC, 2, IBK, AB, P...  124 us
    convert_element_type x1, other arithmetic, shards(): return result.reshape(factors.shape).astype(F32)  6.66 us

profile of v2, /device:TPU:30, one launch (start us, length us, event | category | flops | bytes accessed | tf_op | source)
XLA Modules:
  0.0 130.3 jit_solution(14784661805071857220)
XLA Ops:
  0.0 123.6 %pair_densities.1 = bf16[8,2,16,32,256]{4,3,2,1,0:T(8,128)(2,1)} custom-call(s32[3]{0:T(128)} %i_sub_hbm.1, s32[3]{0:T(128)} %j_row_hbm.1, f32[256]{0:T(256)} %e_occ_hbm.1, f32[8,128]{1,0:T(8,128)} %bitcast.6, bf16[8,2,16,32,256]{4,3,2,1,0:T(8,128)(2,1)} %bitcast.5), custom_call_target="tpu_custom_call" | custom-call | tf_op jit(solution)/shard_map/pair_densities/pallas_call | solution.py:324
  123.6 6.7 %bitcast_convert_fusion = f32[256,32,256]{2,1,0:T(8,128)} fusion(bf16[8,2,16,32,256]{4,3,2,1,0:T(8,128)(2,1)} %pair_densities.1), kind=kLoop, calls=%fused_computation | loop fusion | flops 2097152 | bytes 12582912 | tf_op jit(solution)/shard_map/convert_element_type | solution.py:359

commit v3 on v2

--- a/solution.py
+++ b/solution.py
@@ -20,6 +20,8 @@
 M = KB * AB
 NB = 256
 JB = VIR * AB // NB
+WIDE = 16
+STEP_ORDER = (2, 0, 1)
 FARTOP = 6
 
 
@@ -90,8 +92,9 @@
         pltpu.make_async_copy(ref, ref, rsem).wait()
 
     order = (1, 3, 4, 5, 7, 2, 6)
-    for d in order:
-        send(own_pair, pair.at[:, v, o], gat_s.at[d], gat_r.at[d], (occ_at(d), v))
+    for s in STEP_ORDER:
+        for d in order:
+            send(own_pair.at[s], pair.at[s, v, o], gat_s.at[s, d], gat_r.at[s, d], (occ_at(d), v))
     own_copies = [pltpu.make_async_copy(own_pair, pair.at[:, v, o], loc.at[5])]
     own_copies += [pltpu.make_async_copy(held.at[o, :, pl.ds(c * KB, KB)], rows[c].at[o], loc.at[6 + c]) for c in range(CHUNKS)]
     for copy in own_copies:
@@ -125,7 +128,7 @@
             eb = jnp.where(lax.rem(zb, 2) == 1, e_vir[rb, :], e_turned[rb, :])
             e_group[g, :, high * 128 : (high + 1) * 128] = jnp.where(lane < 64, ea, eb)
 
-    streams = ((1, 0, 0, 8), (2, 0, 0, 8), (0, 0, 0, 8), (0, 1, 0, 8), (2, 1, FARTOP, 8))
+    streams = ((2, 0, 0, 8), (0, 0, 0, 8), (1, 0, 0, 8), (0, 1, 0, 8), (2, 1, FARTOP, 8))
     far_top = {0: 8, 1: 8, 2: FARTOP}
 
     def view(s, b, lo, hi):
@@ -158,17 +161,15 @@
         return hop if direction == 1 else 4 + hop
 
     own_copies[0].wait()
-    for d in range(1, OCC):
-        arrived(pair.at[:, v, occ_from(d)], gat_r.at[d])
-    for s in (0, 2, 1):
-        to_far(s, 0, v, 0, 8)
-    for n in range(3):
+    for n, s in enumerate(STEP_ORDER):
+        for d in range(1, OCC):
+            arrived(pair.at[s, v, occ_from(d)], gat_r.at[s, d])
         for direction in (1, -1):
             to_ring(n, direction, 1, v)
-    for n in range(3):
-        to_mate(n, 0, streams[n][0], v, 0, 8)
+        to_far(s, 0, v, 0, 8)
+        to_mate(n, 0, s, v, 0, 8)
     other = block_at(1, 0)
-    for s, n in ((0, 3), (2, 4), (1, None)):
+    for s, n in ((2, 4), (0, 3), (1, None)):
         arrived(view(s, other, 0, 8), f_r.at[s, 0])
         if n is not None:
             for direction in (1, -1):
@@ -214,11 +215,11 @@
 
     def mate_all(s, hops):
         if s == 0:
-            mate_done(2, hops)
+            mate_done(1, hops)
             mate_done(3, [h for h in hops if h])
             mate_done(4, [h for h in hops if not h])
         else:
-            mate_done(s - 1, hops)
+            mate_done(STEP_ORDER.index(s), hops)
             mate_done(4 + s, hops)
             if s == 2 and FARTOP < 8:
                 mate_done(7, [h for h in hops if h])
@@ -244,40 +245,43 @@
         value = lax.dot_general(left, right, (((1,), (1,)), ((), ())), preferred_element_type=F32)
         amp[s, g] = (-value / (column + e_group[g])).astype(BF16)
 
-    def density(c, s):
-        sub = i_sub[s]
-
-        def part_of(d):
-            r = occ_at(d)
-            left = jnp.concatenate([amp[s, g] for g in range(JB)], axis=1)
-            right = jnp.concatenate([pieces(s, g, r) for g in range(JB)], axis=0)
+    def terms(d, parts):
+        r = occ_at(d)
+        total = [None, None]
+        for s, groups in parts:
+            left = jnp.concatenate([amp[s, g] for g in groups], axis=1)
+            right = jnp.concatenate([pieces(s, g, r) for g in groups], axis=0)
             value = jnp.dot(left, right, preferred_element_type=F32)
-            return [jnp.where(sub == u, value, 0.0) for u in range(2)]
-
-        if s < STEPS - 1:
-            def body(d, carry):
-                for u, term in enumerate(part_of(d)):
-                    acc[u, d] = term if s == 0 else acc[u, d] + term
-                return carry
-
-            lax.fori_loop(0, OCC, body, 0, unroll=4)
-            return
+            for u in range(2):
+                term = jnp.where(i_sub[s] == u, value, 0.0)
+                total[u] = term if total[u] is None else total[u] + term
+        return total
+
+    def add(parts, first):
+        def body(d, carry):
+            for u, term in enumerate(terms(d, parts)):
+                acc[u, d] = term if first else acc[u, d] + term
+            return carry
+
+        lax.fori_loop(0, OCC, body, 0, unroll=2)
+
+    last = []
+
+    def finish(c, parts, held_sum):
         for d in order + (0,):
-            for u, term in enumerate(part_of(d)):
-                snd[c][d, u] = (acc[u, d] + term).astype(BF16).reshape(KB, AB, PB)
+            for u, term in enumerate(terms(d, parts)):
+                value = acc[u, d] + term if held_sum else term
+                snd[c][d, u] = value.astype(BF16).reshape(KB, AB, PB)
                 if d:
                     send(snd[c].at[d, u], out.at[o, u, pl.ds(c * KB, KB)], o_s.at[c, u, d], o_r.at[c, u, d], (occ_at(d), v))
         last.append(pltpu.make_async_copy(snd[c].at[0], out.at[o, :, pl.ds(c * KB, KB)], loc.at[8 + c]))
         last[-1].start()
 
-    last = []
     for hop in range(1, 5):
-        for n in range(5 if FARTOP < 8 else 4):
+        for n in range(5):
             if n == 4 and hop > 1:
                 far_step(1, hop - 1)
             ring_step(n, hop)
-        if FARTOP == 8 and hop > 1:
-            far_step(1, hop - 1)
         if hop > 1:
             far_step(2, hop - 1)
         if hop == 3:
@@ -287,27 +291,30 @@
                 mate_all(s, [1])
             for s, g in ((0, 1), (0, 2), (1, 1), (2, 1)):
                 integrals(0, s, g)
+            add([(0, (1, 2))], True)
     mate_all(0, [3])
     integrals(0, 0, 3)
     for s in (1, 2):
         mate_all(s, [2])
         integrals(0, s, 2)
+    add([(1, (1, 2)), (2, (1, 2))], False)
+    far_step(1, 4)
+    far_step(2, 4)
     mate_all(0, [0, 4])
     integrals(0, 0, 0)
-    far_step(1, 4)
-    far_step(2, 4)
-    density(0, 0)
     for s in (1, 2):
         mate_all(s, [3])
         integrals(0, s, 3)
+    add([(0, (3, 0))], False)
+    for s in (1, 2):
         mate_all(s, [0, 4])
         integrals(0, s, 0)
-        density(0, s)
+    finish(0, [(1, (3, 0)), (2, (3, 0))], True)
     rows_done(1)
     for s in range(STEPS):
         for g in range(JB):
             integrals(1, s, g)
-        density(1, s)
+    finish(1, [(s, tuple(range(JB))) for s in range(STEPS)], False)
     for copy in last:
         copy.wait()
     for c in range(CHUNKS):
@@ -316,6 +323,21 @@
                 arrived(out.at[occ_from(d), u, pl.ds(c * KB, KB)], o_r.at[c, u, d])
     for copy in sends:
         copy.wait_send()
+
+
+def widen(source, out, narrow, wide, in_sem, out_sem):
+    count = source.shape[0] // WIDE
+    parts = [pl.ds(n * count, count) for n in range(WIDE)]
+    ins = [pltpu.make_async_copy(source.at[p], narrow.at[p], in_sem.at[n]) for n, p in enumerate(parts)]
+    outs = [pltpu.make_async_copy(wide.at[p], out.at[p], out_sem.at[n]) for n, p in enumerate(parts)]
+    for copy in ins:
+        copy.start()
+    for n, p in enumerate(parts):
+        ins[n].wait()
+        wide[p] = narrow[p].astype(F32)
+        outs[n].start()
+    for copy in outs:
+        copy.wait()
 
 
 def shards(factors, e_occ, e_vir, i_sub, j_row):
@@ -344,7 +366,7 @@
             pltpu.VMEM((OCC, 2, KB, AB, PB), BF16),
             pltpu.VMEM((OCC, 2, KB, AB, PB), BF16),
             dma((CHUNKS, 2, OCC)), dma((CHUNKS, 2, OCC)),
-            dma((OCC,)), dma((OCC,)),
+            dma((STEPS, OCC)), dma((STEPS, OCC)),
             dma((5, 2, 5)), dma((5, 2, 5)),
             dma((STEPS, 9)), dma((STEPS, 9)),
             dma((8, 9)), dma((8, 9)),
@@ -356,7 +378,19 @@
         ),
         name="pair_densities",
     )(i_sub, j_row, e_occ, e_vir.reshape(8, 128), factors.reshape(OCC, 2, IBK, AB, PB))
-    return result.reshape(factors.shape).astype(F32)
+    return pl.pallas_call(
+        widen,
+        out_shape=jax.ShapeDtypeStruct(factors.shape, F32),
+        in_specs=[hbm],
+        out_specs=hbm,
+        scratch_shapes=[
+            pltpu.VMEM(factors.shape, BF16),
+            pltpu.VMEM(factors.shape, F32),
+            dma((WIDE,)), dma((WIDE,)),
+        ],
+        compiler_params=pltpu.CompilerParams(vmem_limit_bytes=67_043_328),
+        name="widen",
+    )(result.reshape(factors.shape))
 
 
 def solution(mesh):

time: 130 us -> 122 us (0.938)
  the two profiles are of different devices: /device:TPU:30 before, /device:TPU:1 now
where the time goes in v3:
time: 122 us; the launch traced here: 120 us
  Pallas kernels  120 us (98%)
    pallas_call x1, Pallas kernels, shards(): pl.pallas_call(kernel, out_shape=jax.ShapeDtypeStruct((OCC, 2, IBK, AB, P...  115 us
    pallas_call x1, Pallas kernels, shards(): pl.pallas_call(widen, out_shape=jax.ShapeDtypeStruct(factors.shape, F32),...  4.54 us

profile of v3, /device:TPU:1, one launch (start us, length us, event | category | flops | bytes accessed | tf_op | source)
XLA Modules:
  0.0 120.0 jit_solution(10921273319703107019)
XLA Ops:
  0.0 115.2 %pair_densities.1 = bf16[8,2,16,32,256]{4,3,2,1,0:T(8,128)(2,1)} custom-call(s32[3]{0:T(128)} %i_sub_hbm.1, s32[3]{0:T(128)} %j_row_hbm.1, f32[256]{0:T(256)} %e_occ_hbm.1, f32[8,128]{1,0:T(8,128)} %bitcast.5, bf16[8,2,16,32,256]{4,3,2,1,0:T(8,128)(2,1)} %bitcast.4), custom_call_target="tpu_custom_call" | custom-call | tf_op jit(solution)/shard_map/pair_densities/pallas_call | solution.py:346
  115.2 4.5 %widen.1 = f32[256,32,256]{2,1,0:T(8,128)} custom-call(bf16[256,32,256]{2,1,0:T(8,128)(2,1)} %bitcast.3), custom_call_target="tpu_custom_call" | custom-call | tf_op jit(solution)/shard_map/widen/pallas_call | solution.py:381

commit v4 on v3

--- a/solution.py
+++ b/solution.py
@@ -309,20 +309,23 @@
     for s in (1, 2):
         mate_all(s, [0, 4])
         integrals(0, s, 0)
+    gathered, returned = len(sends), 2 * (OCC - 1)
     finish(0, [(1, (3, 0)), (2, (3, 0))], True)
     rows_done(1)
     for s in range(STEPS):
         for g in range(JB):
             integrals(1, s, g)
     finish(1, [(s, tuple(range(JB))) for s in range(STEPS)], False)
+    for copy in sends[:gathered]:
+        copy.wait_send()
     for copy in last:
         copy.wait()
     for c in range(CHUNKS):
+        for copy in sends[gathered + c * returned : gathered + (c + 1) * returned]:
+            copy.wait_send()
         for u in range(2):
             for d in range(1, OCC):
                 arrived(out.at[occ_from(d), u, pl.ds(c * KB, KB)], o_r.at[c, u, d])
-    for copy in sends:
-        copy.wait_send()
 
 
 def widen(source, out, narrow, wide, in_sem, out_sem):

time: 122 us -> 121 us (level)
  no operation moved by 1% of the time
where the time goes in v4:
time: 121 us; the launch traced here: 120 us
  Pallas kernels  119 us (98%)
    pallas_call x1, Pallas kernels, shards(): pl.pallas_call(kernel, out_shape=jax.ShapeDtypeStruct((OCC, 2, IBK, AB, P...  115 us
    pallas_call x1, Pallas kernels, shards(): pl.pallas_call(widen, out_shape=jax.ShapeDtypeStruct(factors.shape, F32),...  4.54 us

profile of v4, /device:TPU:1, one launch (start us, length us, event | category | flops | bytes accessed | tf_op | source)
XLA Modules:
  0.0 119.6 jit_solution(16556653054600521262)
XLA Ops:
  0.0 114.9 %pair_densities.1 = bf16[8,2,16,32,256]{4,3,2,1,0:T(8,128)(2,1)} custom-call(s32[3]{0:T(128)} %i_sub_hbm.1, s32[3]{0:T(128)} %j_row_hbm.1, f32[256]{0:T(256)} %e_occ_hbm.1, f32[8,128]{1,0:T(8,128)} %bitcast.5, bf16[8,2,16,32,256]{4,3,2,1,0:T(8,128)(2,1)} %bitcast.4), custom_call_target="tpu_custom_call" | custom-call | tf_op jit(solution)/shard_map/pair_densities/pallas_call | solution.py:349
  114.9 4.5 %widen.1 = f32[256,32,256]{2,1,0:T(8,128)} custom-call(bf16[256,32,256]{2,1,0:T(8,128)(2,1)} %bitcast.3), custom_call_target="tpu_custom_call" | custom-call | tf_op jit(solution)/shard_map/widen/pallas_call | solution.py:384
